TPU v7x, 256 devices: a whole 4x4x8 slice. The times are simulated.
256 devices in a mesh: rows: 16 (over y, x), cols: 8 (over z), depth: 2 (over core).
Axes of the slice: x: 4, y: 4, z: 8, core: 2. Of those that a mesh axis runs over, the one named last changes fastest.
Arguments:
- tile_left: float32 [16, 8, 64, 2048], P('rows', 'cols'), may hold values from -6 to 6
- tile_right: float32 [16, 8, 64, 2048], P('rows', 'cols'), may hold values from -0.75 to 0.75
- left_u: bfloat16 [2, 16, 16, 64, 2048], P('depth', 'cols', 'rows'), may hold values from -6 to 6
- left_v: bfloat16 [2, 16, 16, 64, 2048], P('depth', 'cols', 'rows'), may hold values from -0.0625 to 0.0625
- rank_left: int32 [2, 16, 16], P('depth', 'cols', 'rows'), may hold values from 16 to 64
- right_u: bfloat16 [2, 16, 8, 64, 2048], P('depth', 'rows', 'cols'), may hold values from -6 to 6
- right_v: bfloat16 [2, 16, 8, 64, 2048], P('depth', 'rows', 'cols'), may hold values from -0.0625 to 0.0625
- rank_right: int32 [2, 16, 8], P('depth', 'rows', 'cols'), may hold values from 16 to 64
- triples: int32 [16, 8, 2, 6], P('rows', 'cols', 'depth'), may hold values from -1 to 15, as said below
Outputs:
- new_left: float32 [16, 8, 64, 2048], P('rows', 'cols', None, 'depth')
- new_right: float32 [16, 8, 64, 2048], P('rows', 'cols', None, 'depth')
Inputs may be any that keep to these rules, and one draw needn't show every extreme that they name: `triples`: for each tile and layer the first entries are distinct panel numbers of 0 to 15 and the remaining entries are -1; every list has at least one panel number, and in every draw some tile in some layer lists all 6.
All inputs are finite; a program needn't handle non-finite values.
Results may differ from a plain program's by a relative error of at most 0.0043.
Values may be sent and summed in bfloat16 or wider, within the bound.
No kernel may reach another device: no remote copies, remote signals or barrier semaphores. Data moves between devices by JAX's collectives and lax.ppermute only.
A program may use at most 128 MiB of HBM per device.

v0:
```python
import math

import jax
import jax.numpy as jnp
from jax import lax
from jax.sharding import PartitionSpec as P

NB = 2048
RK = 64


HIGHEST = lax.Precision.HIGHEST


def swapped(block, axis, apart):
    count = lax.axis_size(axis)
    route = []
    for low in range(count):
        high = low | 1 << apart
        if high != low and high < count:
            route += [(low, high), (high, low)]
    return lax.ppermute(block, axis, route)


def cross(first, second, dim_first, dim_second):
    return lax.dot_general(
        first,
        second,
        (((dim_first,), (dim_second,)), ((), ())),
        precision=HIGHEST,
        preferred_element_type=jnp.float32,
    )


def start_rows(rank, width):
    freq = lax.broadcasted_iota(jnp.int32, (rank, width), 0) + 1
    cell = 2 * lax.broadcasted_iota(jnp.int32, (rank, width), 1) + 1
    phase = freq * cell % (4 * width)
    return jnp.cos(phase.astype(jnp.float32) * (math.pi / (2 * width)))


def orthonormal(rows_t):
    gram = cross(rows_t, rows_t, 1, 1)
    shift = 1e-05 * jnp.trace(gram) / gram.shape[0] + 1e-06
    gram = gram + shift * jnp.eye(gram.shape[0], dtype=gram.dtype)
    lower = lax.linalg.cholesky(gram)
    return lax.linalg.triangular_solve(lower, rows_t, left_side=True, lower=True)


def compress(left_t, right_t):
    probe = start_rows(RK, NB)
    for sweep in range(2):
        first = cross(left_t, probe, 1, 1)
        image = orthonormal(cross(first, right_t, 0, 0))
        second = cross(right_t, image, 1, 1)
        probe = orthonormal(cross(second, left_t, 0, 0))
    first = cross(left_t, probe, 1, 1)
    return (probe, cross(first, right_t, 0, 0))


def slot_term(outer_left, inner_left, rank_l, inner_right, rank_r):
    inner = lax.dot_general(
        inner_left, inner_right, (((1,), (1,)), ((), ())), preferred_element_type=jnp.float32
    )
    index = jnp.arange(RK)
    keep = (index[:, None] < rank_l) & (index[None, :] < rank_r)
    inner = jnp.where(keep, inner, 0.0).astype(jnp.bfloat16)
    return -lax.dot_general(
        inner, outer_left, (((0,), (0,)), ((), ())), preferred_element_type=jnp.float32
    )


def shards(tile_left, tile_right, left_u, left_v, rank_left, right_u, right_v, rank_right, triples):
    layers = lax.axis_size("depth")
    tcols = tile_left.shape[1]
    slots = triples.shape[3]
    row_u, row_v, row_rank = (
        lax.all_gather(left_u, "cols", axis=1, tiled=True),
        lax.all_gather(left_v, "cols", axis=1, tiled=True),
        lax.all_gather(rank_left, "cols", axis=1, tiled=True),
    )
    col_u, col_v, col_rank = (
        lax.all_gather(right_u, "rows", axis=1, tiled=True),
        lax.all_gather(right_v, "rows", axis=1, tiled=True),
        lax.all_gather(rank_right, "rows", axis=1, tiled=True),
    )
    term_list = []
    base_list = []
    tile = 0
    for slot in range(slots):
        panel = triples[0, tile, 0, slot]
        valid = panel >= 0
        chosen = jnp.maximum(panel, 0)
        term_list.append(
            lax.cond(
                valid,
                lambda: slot_term(
                    row_u[0, chosen, 0],
                    row_v[0, chosen, 0],
                    row_rank[0, chosen, 0],
                    col_v[0, chosen, tile],
                    col_rank[0, chosen, tile],
                ),
                lambda: jnp.zeros((RK, NB), jnp.float32),
            )
        )
        base_list.append(
            jnp.where(valid, col_u[0, chosen, tile], jnp.zeros((RK, NB), jnp.bfloat16))
        )
    terms = jnp.stack(term_list).reshape(tcols, slots, RK, NB)
    bases = jnp.stack(base_list).reshape(tcols, slots, RK, NB)
    probes = []
    images = []
    tile = 0
    left_t = jnp.concatenate(
        [tile_left[0, tile] / layers, terms[tile].reshape(slots * RK, NB)], axis=0
    )
    right_t = jnp.concatenate(
        [tile_right[0, tile], bases[tile].astype(jnp.float32).reshape(slots * RK, NB)], axis=0
    )
    probe, image = compress(left_t, right_t)
    probes.append(probe)
    images.append(image)
    probes = jnp.stack(probes)
    images = jnp.stack(images)
    layer_index = lax.axis_index("depth")
    other_probes, other_images = swapped((probes, images), "depth", 0)
    lower_side = layer_index >> 0 & 1 == 0
    first_probes = jnp.where(lower_side, probes, other_probes)
    second_probes = jnp.where(lower_side, other_probes, probes)
    first_images = jnp.where(lower_side, images, other_images)
    second_images = jnp.where(lower_side, other_images, images)
    tile = 0
    probe, image = compress(
        jnp.concatenate([first_probes[tile], second_probes[tile]], axis=0),
        jnp.concatenate([first_images[tile], second_images[tile]], axis=0),
    )
    joined_probes = [probe]
    joined_images = [image]
    probes = jnp.stack(joined_probes)
    images = jnp.stack(joined_images)
    share = NB // layers
    offset = layer_index * share
    new_left = lax.dynamic_slice_in_dim(probes * math.sqrt(NB), offset, share, 2).reshape(
        1, tcols, RK, share
    )
    new_right = lax.dynamic_slice_in_dim(images / math.sqrt(NB), offset, share, 2).reshape(
        1, tcols, RK, share
    )
    return (new_left, new_right)


def solution(mesh):
    in_specs = (
        P("rows", "cols", None, None),
        P("rows", "cols", None, None),
        P("depth", "cols", "rows", None, None),
        P("depth", "cols", "rows", None, None),
        P("depth", "cols", "rows"),
        P("depth", "rows", "cols", None, None),
        P("depth", "rows", "cols", None, None),
        P("depth", "rows", "cols"),
        P("rows", "cols", "depth", None),
    )
    out_specs = (P("rows", "cols", None, "depth"), P("rows", "cols", None, "depth"))
    return jax.shard_map(shards, mesh=mesh, in_specs=in_specs, out_specs=out_specs, check_vma=False)
```

profile of v0, /device:TPU:101, one launch (start us, length us, event | category | flops | bytes accessed | tf_op | source)
XLA Modules:
  0.0 456.9 jit_solution(14910221890863665000)
XLA Ops:
  12.6 10.6 %all-reduce.1 = s32[16]{0:T(128)S(1)} all-reduce(s32[16]{0:T(128)S(1)} %bitcast_dynamic-update-slice_fusion.6), channel_id=1, replica_groups=mesh['rows'=16,'cols'=8,'depth'=2] {'rows'}, use_global_device_ids=true, to_apply=%add.1 | all-reduce | flops 16 | bytes 128
  35.1 11.8 %all-reduce = s32[16]{0:T(128)S(1)} all-reduce(s32[16]{0:T(128)S(1)} %bitcast_dynamic-update-slice_fusion.7), channel_id=1, replica_groups=mesh['rows'=16,'cols'=8,'depth'=2] {'cols'}, use_global_device_ids=true, to_apply=%add | all-reduce | flops 16 | bytes 128
  48.8 17.0 %all-gather.5.cloned.1.call-done = bf16[1,16,1,64,2048]{4,3,2,0,1:T(8,128)(2,1)} async-done(((bf16[1,2,1,64,2048]{4,3,2,0,1:T(8,128)(2,1)}), bf16[1,16,1,64,2048]{4,3,2,0,1:T(8,128)(2,1)}) %all-gather.5.cloned.1.call-update) | async-done | bytes 4194320 | tf_op jit(solution)/shard_map/all_gather | solution.py:79
  65.8 55.3 %all-gather.9.cloned.1.call-done = bf16[1,16,1,64,2048]{4,3,2,0,1:T(8,128)(2,1)} async-done(((bf16[1,2,1,64,2048]{4,3,2,0,1:T(8,128)(2,1)}), bf16[1,16,1,64,2048]{4,3,2,0,1:T(8,128)(2,1)}) %all-gather.9.cloned.1.call-update) | async-done | bytes 4194320 | tf_op jit(solution)/shard_map/all_gather | solution.py:78
  121.2 58.1 %all-gather.7.cloned.1.call-done = bf16[1,16,1,64,2048]{4,3,2,0,1:T(8,128)(2,1)} async-done(((bf16[1,1,1,64,2048]{4,3,2,0,1:T(8,128)(2,1)}), bf16[1,16,1,64,2048]{4,3,2,0,1:T(8,128)(2,1)}) %all-gather.7.cloned.1.call-update) | async-done | bytes 4194320 | tf_op jit(solution)/shard_map/all_gather | solution.py:84
  179.2 3.5 conditional.6
  183.6 54.2 %all-gather.11.cloned.1.call-done = bf16[1,16,1,64,2048]{4,3,2,0,1:T(8,128)(2,1)} async-done(((bf16[1,1,1,64,2048]{4,3,2,0,1:T(8,128)(2,1)}), bf16[1,16,1,64,2048]{4,3,2,0,1:T(8,128)(2,1)}) %all-gather.11.cloned.1.call-update) | async-done | bytes 4194320 | tf_op jit(solution)/shard_map/all_gather | solution.py:83
  244.2 4.4 conditional.7
  246.1 2.5 fusion.19
  248.7 1.9 constant_dynamic-update-slice_fusion.4
  250.5 4.4 conditional.8
  252.4 2.5 fusion.38
  254.9 1.9 constant_dynamic-update-slice_fusion.3
  256.8 4.4 conditional.9
  258.7 2.5 fusion.57
  261.2 1.9 constant_dynamic-update-slice_fusion.2
  263.2 4.4 conditional.10
  265.1 2.5 fusion.76
  267.6 1.9 constant_dynamic-update-slice_fusion.1
  270.5 2.0 constant_dynamic-update-slice_fusion
  272.4 6.8 %fusion.122 = f32[448,64]{1,0:T(8,128)S(1)} fusion(f32[384,2048]{1,0:T(8,128)} %bitcast.304, f32[64,2048]{1,0:T(8,128)} %multiply_bitcast_fusion, s32[2048]{0:T(1024)S(1)} %multiply_add_fusion, s32[64]{0:T(128)S(1)} %iota_add_fusion), kind=kOutput, calls=%fused_computation.132 | convolution fusion | flops 707395584 | bytes 3793152 | tf_op jit(solution)/shard_map/dot_general | solution.py:26
  279.3 2.4 fusion.117
  284.4 5.8 %custom-call.20 = f32[64,64]{1,0:T(8,128)S(1)} custom-call(f32[64,64]{1,0:T(8,128)S(1)} %fusion.180), custom_call_target="Cholesky" | custom-call | tf_op jit(solution)/shard_map/cholesky/custom-call.1 | solution.py:46
  291.6 4.9 %custom-call.21 = f32[1,64,64]{1,2,0:T(8,128)S(1)} custom-call(f32[1,64,64]{2,1,0:T(8,128)S(1)} %fusion.141), custom_call_target="InvertDiagBlocksLowerTriangular" | custom-call | tf_op jit(solution)/shard_map/triangular_solve/custom-call.0 | solution.py:47
  298.4 4.5 fusion.116
  302.9 2.4 fusion.121
  308.0 5.8 %custom-call.22 = f32[64,64]{1,0:T(8,128)S(1)} custom-call(f32[64,64]{1,0:T(8,128)S(1)} %fusion.176), custom_call_target="Cholesky" | custom-call | tf_op jit(solution)/shard_map/cholesky/custom-call.1 | solution.py:46
  315.2 4.9 %custom-call.23 = f32[1,64,64]{1,2,0:T(8,128)S(1)} custom-call(f32[1,64,64]{2,1,0:T(8,128)S(1)} %fusion.142), custom_call_target="InvertDiagBlocksLowerTriangular" | custom-call | tf_op jit(solution)/shard_map/triangular_solve/custom-call.0 | solution.py:47
  321.8 5.0 %fusion.120 = f32[448,64]{1,0:T(8,128)S(1)} fusion(f32[64,2048]{1,0:T(8,128)S(1)} %fusion.173, f32[384,2048]{1,0:T(8,128)} %bitcast.305, f32[64,2048]{1,0:T(8,128)} %multiply_bitcast_fusion), kind=kOutput, calls=%fused_computation.130 | convolution fusion | flops 705560576 | bytes 4308992 | tf_op jit(solution)/shard_map/dot_general | solution.py:26
  326.8 2.4 fusion.115
  332.0 6.0 %custom-call.24 = f32[64,64]{1,0:T(8,128)S(1)} custom-call(f32[64,64]{1,0:T(8,128)S(1)} %fusion.172), custom_call_target="Cholesky" | custom-call | tf_op jit(solution)/shard_map/cholesky/custom-call.1 | solution.py:46
  339.3 4.9 %custom-call.25 = f32[1,64,64]{1,2,0:T(8,128)S(1)} custom-call(f32[1,64,64]{2,1,0:T(8,128)S(1)} %fusion.143), custom_call_target="InvertDiagBlocksLowerTriangular" | custom-call | tf_op jit(solution)/shard_map/triangular_solve/custom-call.0 | solution.py:47
  346.0 4.0 fusion.114
  350.1 2.4 fusion.119
  355.2 5.8 %custom-call.26 = f32[64,64]{1,0:T(8,128)S(1)} custom-call(f32[64,64]{1,0:T(8,128)S(1)} %fusion.168), custom_call_target="Cholesky" | custom-call | tf_op jit(solution)/shard_map/cholesky/custom-call.1 | solution.py:46
  362.4 4.9 %custom-call.27 = f32[1,64,64]{1,2,0:T(8,128)S(1)} custom-call(f32[1,64,64]{2,1,0:T(8,128)S(1)} %fusion.144), custom_call_target="InvertDiagBlocksLowerTriangular" | custom-call | tf_op jit(solution)/shard_map/triangular_solve/custom-call.0 | solution.py:47
  367.3 2.5 fusion.165
  370.6 5.2 %fusion.118 = f32[448,64]{1,0:T(8,128)S(1)} fusion(f32[64,2048]{1,0:T(8,128)} %fusion.165, f32[384,2048]{1,0:T(8,128)} %bitcast.306, f32[64,2048]{1,0:T(8,128)} %multiply_bitcast_fusion), kind=kOutput, calls=%fused_computation.128 | convolution fusion | flops 705560576 | bytes 4308992 | tf_op jit(solution)/shard_map/dot_general | solution.py:26
  375.9 2.4 convolution_bitcast_fusion
  380.1 3.0 fusion.131
  385.8 5.8 %custom-call.28 = f32[64,64]{1,0:T(8,128)S(1)} custom-call(f32[64,64]{1,0:T(8,128)S(1)} %fusion.164), custom_call_target="Cholesky" | custom-call | tf_op jit(solution)/shard_map/cholesky/custom-call.1 | solution.py:46
  393.0 4.9 %custom-call.29 = f32[1,64,64]{1,2,0:T(8,128)S(1)} custom-call(f32[1,64,64]{2,1,0:T(8,128)S(1)} %fusion.145), custom_call_target="InvertDiagBlocksLowerTriangular" | custom-call | tf_op jit(solution)/shard_map/triangular_solve/custom-call.0 | solution.py:47
  402.1 5.8 %custom-call.30 = f32[64,64]{1,0:T(8,128)S(1)} custom-call(f32[64,64]{1,0:T(8,128)S(1)} %fusion.160), custom_call_target="Cholesky" | custom-call | tf_op jit(solution)/shard_map/cholesky/custom-call.1 | solution.py:46
  409.3 4.9 %custom-call.31 = f32[1,64,64]{1,2,0:T(8,128)S(1)} custom-call(f32[1,64,64]{2,1,0:T(8,128)S(1)} %fusion.146), custom_call_target="InvertDiagBlocksLowerTriangular" | custom-call | tf_op jit(solution)/shard_map/triangular_solve/custom-call.0 | solution.py:47
  418.6 5.8 %custom-call.32 = f32[64,64]{1,0:T(8,128)S(1)} custom-call(f32[64,64]{1,0:T(8,128)S(1)} %fusion.156), custom_call_target="Cholesky" | custom-call | tf_op jit(solution)/shard_map/cholesky/custom-call.1 | solution.py:46
  425.8 4.9 %custom-call.33 = f32[1,64,64]{1,2,0:T(8,128)S(1)} custom-call(f32[1,64,64]{2,1,0:T(8,128)S(1)} %fusion.147), custom_call_target="InvertDiagBlocksLowerTriangular" | custom-call | tf_op jit(solution)/shard_map/triangular_solve/custom-call.0 | solution.py:47
  435.0 5.8 %custom-call.34 = f32[64,64]{1,0:T(8,128)S(1)} custom-call(f32[64,64]{1,0:T(8,128)S(1)} %fusion.152), custom_call_target="Cholesky" | custom-call | tf_op jit(solution)/shard_map/cholesky/custom-call.1 | solution.py:46
  442.1 4.9 %custom-call.35 = f32[1,64,64]{1,2,0:T(8,128)S(1)} custom-call(f32[1,64,64]{2,1,0:T(8,128)S(1)} %fusion.148), custom_call_target="InvertDiagBlocksLowerTriangular" | custom-call | tf_op jit(solution)/shard_map/triangular_solve/custom-call.0 | solution.py:47
  (137 shorter events, 73.1 us)
Async XLA Ops:
  7.2 58.6 %all-gather.5.cloned.1.call-start = ((), (), s32[]{:S(2)}) async-start(), calls=%async_computation | async-start | bytes 4718592 | tf_op jit(solution)/shard_map/all_gather | solution.py:79
  7.9 113.3 %all-gather.9.cloned.1.call-start = ((), (), s32[]{:S(2)}) async-start(), calls=%async_computation.2 | async-start | bytes 4718592 | tf_op jit(solution)/shard_map/all_gather | solution.py:78
  8.6 170.6 %all-gather.7.cloned.1.call-start = ((), (), s32[]{:S(2)}) async-start(), calls=%async_computation.1 | async-start | bytes 4456448 | tf_op jit(solution)/shard_map/all_gather | solution.py:84
  9.4 228.3 %all-gather.11.cloned.1.call-start = ((), (), s32[]{:S(2)}) async-start(), calls=%async_computation.3 | async-start | bytes 4456448 | tf_op jit(solution)/shard_map/all_gather | solution.py:83
  270.5 8.8 %copy-start.2 = (f32[1,1,64,2048]{3,2,1,0:T(8,128)S(1)}, f32[1,1,64,2048]{3,2,1,0:T(8,128)}, u32[]{:S(2)}) copy-start(f32[1,1,64,2048]{3,2,1,0:T(8,128)} %param.25) | copy-start | bytes 1572868
  281.7 0.8 copy-start.7
  296.5 6.3 %copy-start = (f32[6,64,2048]{2,1,0:T(8,128)S(1)}, f32[6,64,2048]{2,1,0:T(8,128)}, u32[]{:S(2)}) copy-start(f32[6,64,2048]{2,1,0:T(8,128)} %constant_dynamic-update-slice_fusion) | copy-start | bytes 9437188
  296.5 6.3 %copy-start.5 = (f32[64,2048]{1,0:T(8,128)S(1)}, f32[64,2048]{1,0:T(8,128)}, u32[]{:S(2)}) copy-start(f32[64,2048]{1,0:T(8,128)} %multiply_bitcast_fusion) | copy-start | bytes 1572868
  305.3 0.8 copy-start.8
  320.1 6.7 %copy-start.3 = (f32[1,1,64,2048]{3,2,1,0:T(8,128)S(1)}, f32[1,1,64,2048]{3,2,1,0:T(8,128)}, u32[]{:S(2)}) copy-start(f32[1,1,64,2048]{3,2,1,0:T(8,128)} %param.25) | copy-start | bytes 1572868
  329.2 0.8 copy-start.9
  344.2 5.9 %copy-start.1 = (f32[6,64,2048]{2,1,0:T(8,128)S(1)}, f32[6,64,2048]{2,1,0:T(8,128)}, u32[]{:S(2)}) copy-start(f32[6,64,2048]{2,1,0:T(8,128)} %constant_dynamic-update-slice_fusion) | copy-start | bytes 9437188
  344.2 5.9 %copy-start.6 = (f32[64,2048]{1,0:T(8,128)S(1)}, f32[64,2048]{1,0:T(8,128)}, u32[]{:S(2)}) copy-start(f32[64,2048]{1,0:T(8,128)} %multiply_bitcast_fusion) | copy-start | bytes 1572868
  352.5 0.8 copy-start.10
  369.8 9.0 %collective-permute-start.1 = (f32[1,64,2048]{2,1,0:T(8,128)}, f32[1,64,2048]{2,1,0:T(8,128)}, u32[]{:S(2)}, u32[]{:S(2)}) collective-permute-start(f32[1,64,2048]{2,1,0:T(8,128)} %bitcast.107), channel_id=1, source_target_pairs={{0,1},{1,0},{2,3},{3,2},{4,5},{5,4},{6,7},{7,6},{8,9},{9,8},{10,11... | collective-permute-start | bytes 1572872 | tf_op jit(solution)/shard_map/ppermute | solution.py:22
  370.6 5.2 %copy-start.4 = (f32[1,1,64,2048]{3,2,1,0:T(8,128)S(1)}, f32[1,1,64,2048]{3,2,1,0:T(8,128)}, u32[]{:S(2)}) copy-start(f32[1,1,64,2048]{3,2,1,0:T(8,128)} %param.25) | copy-start | bytes 1572868
  378.3 4.8 %collective-permute-start = (f32[1,64,2048]{2,1,0:T(8,128)S(1)}, f32[1,64,2048]{2,1,0:T(8,128)S(1)}, u32[]{:S(2)}, u32[]{:S(2)}) collective-permute-start(f32[1,64,2048]{2,1,0:T(8,128)S(1)} %convolution_bitcast_fusion), channel_id=1, source_target_pairs={{0,1},{1,0},{2,3},{3,2},{4,5},{5,4},{6,7},{7,6},{8,9},{9,8},{10,11... | collective-permute-start | bytes 1572872 | tf_op jit(solution)/shard_map/ppermute | solution.py:22
Sparse Core Ops, SparseCore 0:
  9.8 56.0 all-gather.4
  67.6 53.5 all-gather.8
  123.6 55.5 all-gather.6
  181.5 56.1 all-gather.10
where the time goes:
time: 465 us; the launch traced here: 457 us
  waiting for transfers between devices  187 us (40%)
  other arithmetic  114 us (25%)
  matrix products  79.4 us (17%)
  between operations  28.9 us (6%)
  local copies, waits for them, and re-layouts  23.4 us (5%)
  blocking collectives  22.4 us (5%)
    all_gather x1, waiting for transfers between devices, shards(): lax.all_gather(right_v, 'rows', axis=1, tiled=True)  58.1 us
    dot_general x28, matrix products, cross(): lax.dot_general(first, second, (((dim_first,), (dim_second,)), ((), ())),...  57.3 us
    all_gather x1, waiting for transfers between devices, shards(): lax.all_gather(left_u, 'cols', axis=1, tiled=True)  55.3 us
    all_gather x1, waiting for transfers between devices, shards(): lax.all_gather(right_u, 'rows', axis=1, tiled=True)  54.2 us
    another operation x24, other arithmetic, orthonormal(): lower = lax.linalg.cholesky(gram)  52.3 us
    another operation x16, other arithmetic, orthonormal(): lax.linalg.triangular_solve(lower, rows_t, left_side=True, lower=True)  44.4 us
    unnamed x2, blocking collectives  22.4 us
    all_gather x1, waiting for transfers between devices, shards(): lax.all_gather(left_v, 'cols', axis=1, tiled=True)  17 us
  transfers between devices with their start and end apart: 6, of which 4 were waited for; matrix products, arithmetic and copies ran while one was open for 5% of the time, Pallas kernels for 0%

commit v1 on v0

v1 whole, which is shorter than its diff:
```python
import math

import jax
import jax.numpy as jnp
from jax import lax
from jax.experimental import pallas as pl
from jax.experimental.pallas import tpu as pltpu
from jax.sharding import PartitionSpec as P

NB = 2048
RK = 64
BF = jnp.bfloat16
F32 = jnp.float32


def nt(first, second):
    return lax.dot_general(
        first, second, (((1,), (1,)), ((), ())), preferred_element_type=F32
    )


def nn(first, second):
    return lax.dot_general(
        first, second, (((1,), (0,)), ((), ())), preferred_element_type=F32
    )


def halves(x):
    high = x.astype(BF)
    return high, (x - high.astype(F32)).astype(BF)


def start_pair():
    rows = start_rows(RK, NB)
    high = lax.reduce_precision(rows, 8, 7)
    return jnp.concatenate([high, rows - high], axis=0).astype(BF)


def product(mul, first, second):
    a, b = halves(first), halves(second)
    return mul(a[0], b[0]) + (mul(a[0], b[1]) + mul(a[1], b[0]))


def start_rows(rank, width):
    freq = lax.broadcasted_iota(jnp.int32, (rank, width), 0) + 1
    cell = 2 * lax.broadcasted_iota(jnp.int32, (rank, width), 1) + 1
    phase = freq * cell % (4 * width)
    return jnp.cos(phase.astype(F32) * (math.pi / (2 * width)))


def spread(x, lane):
    return jnp.broadcast_to(x[:, lane : lane + 1], (8, 128))


def factor_inverse(full):
    v = [full[8 * b : 8 * b + 8] for b in range(8)]
    sub = lax.broadcasted_iota(jnp.int32, (8, 128), 0)
    out = []
    for b in range(8):
        at = 8 * b
        rows = [jnp.broadcast_to(v[b][p : p + 1], (8, 128)) for p in range(8)]
        s = [[spread(rows[p], at + q) for q in range(p + 1)] for p in range(8)]
        low = [[None] * 8 for _ in range(8)]
        n, inv = [], []
        for p in range(8):
            d = s[p][p]
            y = lax.rsqrt(d)
            y = y * (1.5 - 0.5 * d * y * y)
            inv.append(y)
            n.append(rows[p] * y)
            for q in range(p + 1, 8):
                low[q][p] = s[q][p] * y
            for q in range(p + 1, 8):
                for r in range(p + 1, q + 1):
                    s[q][r] = s[q][r] - low[q][p] * low[r][p]
                rows[q] = rows[q] - low[q][p] * n[p]
        block = n[0]
        for p in range(1, 8):
            block = jnp.where(sub == p, n[p], block)
        out.append(block)
        if b < 7:
            t = [None] * 8
            for q in reversed(range(8)):
                acc = n[q]
                for p in range(q + 1, 8):
                    acc = acc - low[p][q] * t[p]
                t[q] = acc * inv[q]
            for below in range(b + 1, 8):
                acc = v[below]
                for q in range(8):
                    acc = acc - spread(v[below], at + q) * t[q]
                v[below] = acc
    return jnp.concatenate(out, axis=0)


def masks():
    row = lax.broadcasted_iota(jnp.int32, (RK, 2 * RK), 0)
    col = lax.broadcasted_iota(jnp.int32, (RK, 2 * RK), 1)
    return row == col, row + RK == col, col >= RK


def sweeps(left_gram, right_gram, z):
    diag, unit, upper = masks()
    n = z.shape[1]
    gz = product(nn, z, right_gram)
    for half in range(4):
        after = left_gram if half % 2 == 0 else right_gram
        gram = product(nt, z, jnp.concatenate([gz, jnp.zeros((RK, n), F32)], axis=0))
        trace = jnp.sum(jnp.where(diag, gram, 0.0), keepdims=True)
        shift = 1e-05 * trace / RK + 1e-06
        full = jnp.where(diag, gram + shift, gram)
        full = jnp.where(unit, 1.0, full)
        if half < 3:
            ahead = product(nn, gz, after)
        inverse = jnp.where(upper, factor_inverse(full), 0.0)
        if half < 3:
            both = jnp.concatenate([gz, ahead], axis=1)
            both = product(nn, inverse, jnp.concatenate([both, both], axis=0))
            z, gz = both[:, :n], both[:, n:]
        else:
            both = jnp.concatenate([z, gz], axis=1)
            both = product(nn, inverse, jnp.concatenate([both, both], axis=0))
            return both[:, :n], both[:, n:]


def layer_kernel(
    triples, tile_left, tile_right, inner, start, left_u, right_u, probe, image, w, r, d, sems
):
    copies = []
    for slot in range(6):
        chosen = jnp.maximum(triples[slot], 0)
        for side, (src, dst) in enumerate(((left_u, w), (right_u, r))):
            copy = pltpu.make_async_copy(
                src.at[chosen], dst.at[pl.ds(RK * slot, RK)], sems.at[side, slot]
            )
            copy.start()
            copies.append(copy)
    w[384:448], w[448:512] = halves(tile_left[...])
    r[384:448], r[448:512] = halves(tile_right[...])
    row = lax.broadcasted_iota(jnp.int32, (128, 128), 0)
    col = lax.broadcasted_iota(jnp.int32, (128, 128), 1)
    d[...] = jnp.zeros_like(d)
    for slot in range(6):
        panel = triples[slot]
        value = -inner[jnp.maximum(panel, 0)]
        value = jnp.where(panel >= 0, value, jnp.zeros_like(value))
        at = RK * (slot % 2)
        d[slot // 2, at : at + RK, at : at + RK] = value
    d[3] = jnp.where((row - col) % RK == 0, 0.5, 0.0).astype(BF)
    for copy in copies:
        copy.wait()
    left = w[...]
    right = r[...]
    right_gram = nt(right, right)
    raw = nt(left, left)
    z = nt(start[...], left)
    z = z[:RK] + z[RK:]
    mixed = []
    for t in range(4):
        high, low = halves(raw[128 * t : 128 * t + 128])
        mixed.append(nn(d[t], high) + nn(d[t], low))
    mixed = jnp.concatenate(mixed + [z], axis=0)
    high, low = halves(mixed)
    out = []
    for t in range(4):
        cut = slice(128 * t, 128 * t + 128)
        out.append(nt(high[:, cut], d[t]) + nt(low[:, cut], d[t]))
    out = jnp.concatenate(out, axis=1)
    x, y = sweeps(out[:512], right_gram, out[512:])
    high, low = halves(x)
    out = []
    for t in range(4):
        cut = slice(128 * t, 128 * t + 128)
        out.append(nn(high[:, cut], d[t]) + nn(low[:, cut], d[t]))
    high, low = halves(jnp.concatenate(out, axis=1))
    probe[...] = nn(high, left) + nn(low, left)
    high, low = halves(y)
    image[...] = nn(high, right) + nn(low, right)


def layer_update(triples, tile_left, tile_right, inner, start, left_u, right_u):
    vmem = pl.BlockSpec(memory_space=pltpu.VMEM)
    hbm = pl.BlockSpec(memory_space=pl.ANY)
    return pl.pallas_call(
        layer_kernel,
        out_shape=[jax.ShapeDtypeStruct((RK, NB), F32)] * 2,
        in_specs=[pl.BlockSpec(memory_space=pltpu.SMEM), vmem, vmem, vmem, vmem, hbm, hbm],
        out_specs=[vmem, vmem],
        scratch_shapes=[
            pltpu.VMEM((512, NB), BF),
            pltpu.VMEM((512, NB), BF),
            pltpu.VMEM((4, 128, 128), BF),
            pltpu.SemaphoreType.DMA((2, 6)),
        ],
        compiler_params=pltpu.CompilerParams(vmem_limit_bytes=40 << 20),
        name="layer_update",
    )(triples, tile_left, tile_right, inner, start, left_u, right_u)


def join_kernel(offset, probes_a, probes_b, images_a, images_b, start, new_left, new_right, w, r):
    for store, first, second in ((w, probes_a, probes_b), (r, images_a, images_b)):
        store[0:64], store[128:192] = halves(first[...])
        store[64:128], store[192:256] = halves(second[...])

    def folded(x):
        return (x[:128, :128] + x[128:, 128:]) + (x[:128, 128:] + x[128:, :128])

    left = w[...]
    right = r[...]
    z = nt(start[...], left)
    z = z[:RK] + z[RK:]
    z = z[:, :128] + z[:, 128:]
    x, y = sweeps(folded(nt(left, left)), folded(nt(right, right)), z)
    share = new_left.shape[1]
    cut = pl.ds(pl.multiple_of(offset[0], share), share)
    for store, coefs, out, scale in (
        (w, x, new_left, math.sqrt(NB)),
        (r, y, new_right, 1.0 / math.sqrt(NB)),
    ):
        high, low = halves(coefs)
        out[...] = scale * (
            nn(high, store[0:128, cut])
            + (nn(high, store[128:256, cut]) + nn(low, store[0:128, cut]))
        )


def join(offset, probes_a, probes_b, images_a, images_b, start, share):
    vmem = pl.BlockSpec(memory_space=pltpu.VMEM)
    return pl.pallas_call(
        join_kernel,
        out_shape=[jax.ShapeDtypeStruct((RK, share), F32)] * 2,
        in_specs=[pl.BlockSpec(memory_space=pltpu.SMEM)] + [vmem] * 5,
        out_specs=[vmem, vmem],
        scratch_shapes=[pltpu.VMEM((256, NB), BF), pltpu.VMEM((256, NB), BF)],
        compiler_params=pltpu.CompilerParams(vmem_limit_bytes=40 << 20),
        name="join",
    )(offset, probes_a, probes_b, images_a, images_b, start)


def gathered(left_u, right_u):
    return (
        lax.all_gather(left_u, "cols", axis=0, tiled=True),
        lax.all_gather(right_u, "rows", axis=0, tiled=True),
    )


def inners(left_v, rank_left, right_v, rank_right):
    index = lax.broadcasted_iota(jnp.int32, (RK, 1), 0)
    left_v = jnp.where(index[None] < rank_left[:, None, None], left_v, 0)
    right_v = jnp.where(index < rank_right[0], right_v, 0)
    route = []
    for r in range(16):
        for c in range(8):
            route.append((r * 8 + c, ((r % 2) * 8 + c) * 8 + r // 2))
    right_v = lax.ppermute(right_v, ("rows", "cols"), route)
    right_v = lax.all_gather(right_v, "rows").reshape(2, 8 * RK, NB)
    inner = lax.dot_general(
        right_v, left_v, (((2,), (2,)), ((0,), (0,))), preferred_element_type=F32
    ).astype(BF)
    inner = inner.reshape(2, 8, RK, RK).transpose(1, 0, 2, 3)
    return lax.all_to_all(inner, "cols", 0, 0).reshape(16, RK, RK)


def shards(tile_left, tile_right, left_u, left_v, rank_left, right_u, right_v, rank_right, triples):
    inner = inners(left_v[0, :, 0], rank_left[0, :, 0], right_v[0, 0, 0], rank_right[0, 0])
    row_u, col_u = gathered(left_u[0, :, 0], right_u[0, :, 0])
    start = start_pair()
    probe, image = layer_update(
        triples[0, 0, 0], tile_left[0, 0], tile_right[0, 0], inner, start, row_u, col_u
    )
    layer = lax.axis_index("depth")
    other_probe, other_image = lax.ppermute((probe, image), "depth", [(0, 1), (1, 0)])
    share = NB // 2
    lower = layer == 0
    new_left, new_right = join(
        (layer * share).astype(jnp.int32).reshape(1),
        jnp.where(lower, probe, other_probe),
        jnp.where(lower, other_probe, probe),
        jnp.where(lower, image, other_image),
        jnp.where(lower, other_image, image),
        start,
        share,
    )
    return new_left.reshape(1, 1, RK, share), new_right.reshape(1, 1, RK, share)


def solution(mesh):
    in_specs = (
        P("rows", "cols", None, None),
        P("rows", "cols", None, None),
        P("depth", "cols", "rows", None, None),
        P("depth", "cols", "rows", None, None),
        P("depth", "cols", "rows"),
        P("depth", "rows", "cols", None, None),
        P("depth", "rows", "cols", None, None),
        P("depth", "rows", "cols"),
        P("rows", "cols", "depth", None),
    )
    out_specs = (P("rows", "cols", None, "depth"), P("rows", "cols", None, "depth"))
    return jax.shard_map(shards, mesh=mesh, in_specs=in_specs, out_specs=out_specs, check_vma=False)
```

time: 465 us -> 276 us (0.59); the launches traced: 457 us -> 273 us
  other arithmetic: 114 us -> 5.19 us
  matrix products: 79.4 us -> 3.7 us
  Pallas kernels: 0 us -> 35.9 us
  blocking collectives: 22.4 us -> 0 us
  local copies, waits for them, and re-layouts: 23.4 us -> 6.62 us
  between operations: 28.9 us -> 14.5 us
  waiting for transfers between devices: 187 us -> 197 us
  starting transfers between devices: 1.49 us -> 10 us
    another operation x41 -> x1, other arithmetic: 97.7 us -> 2.13 us  [the longest x24 52.3 us: orthonormal(): lower = lax.linalg.cholesky(gram)]
    dot_general x33 -> x1, matrix products: 69 us -> 3.7 us  [inners(): lax.dot_general(right_v, left_v, (((2,), (2,)), ((0,), (0,))), preferred_...]
    pallas_call x0 -> x2, Pallas kernels: none -> 35.9 us  [the longest x1 20.7 us: layer_update(): pl.pallas_call(layer_kernel, out_shape=[jax.ShapeDtypeStruct((RK, NB), F3...]
    unnamed x2 -> x0, blocking collectives: 22.4 us -> none
    ppermute x2 -> x3, waiting for transfers between devices: 0.01 us -> 22 us  [the longest x1 20.4 us: inners(): right_v = lax.ppermute(right_v, ('rows', 'cols'), route)]
    all_gather x4 -> x3, waiting for transfers between devices: 185 us -> 169 us  [the longest x1 71.6 us: inners(): right_v = lax.all_gather(right_v, 'rows').reshape(2, 8 * RK, NB)]
    another operation x8 -> x0, matrix products: 10.4 us -> none  [orthonormal(): lax.linalg.triangular_solve(lower, rows_t, left_side=True, lower=True)]
    unnamed x33 -> x14, local copies, waits for them, and re-layouts: 15.5 us -> 6.19 us
  transfers between devices with their start and end apart: 6 -> 7, of which waited for: 4 -> 6; matrix products, arithmetic and copies ran while one was open for 5% -> 3% of each run, Pallas kernels for 0% -> 0%
where the time goes in v1:
time: 276 us; the launch traced here: 273 us
  waiting for transfers between devices  197 us (71%)
  Pallas kernels  35.9 us (13%)
  between operations  14.5 us (5%)
  starting transfers between devices  10 us (4%)
  local copies, waits for them, and re-layouts  6.62 us (2%)
  other arithmetic  5.19 us (2%)
  matrix products  3.7 us (1%)
    all_gather x1, waiting for transfers between devices, inners(): right_v = lax.all_gather(right_v, 'rows').reshape(2, 8 * RK, NB)  71.6 us
    all_gather x1, waiting for transfers between devices, gathered(): lax.all_gather(right_u, 'rows', axis=0, tiled=True)  56.3 us
    all_gather x1, waiting for transfers between devices, gathered(): lax.all_gather(left_u, 'cols', axis=0, tiled=True)  40.6 us
    pallas_call x1, Pallas kernels, layer_update(): pl.pallas_call(layer_kernel, out_shape=[jax.ShapeDtypeStruct((RK, NB), F3...  20.7 us
    ppermute x1, waiting for transfers between devices, inners(): right_v = lax.ppermute(right_v, ('rows', 'cols'), route)  20.4 us
    pallas_call x1, Pallas kernels, join(): pl.pallas_call(join_kernel, out_shape=[jax.ShapeDtypeStruct((RK, share),...  15.2 us
    all_to_all x1, starting transfers between devices, inners(): return lax.all_to_all(inner, 'cols', 0, 0).reshape(16, RK, RK)  6.74 us
    unnamed x14, local copies, waits for them, and re-layouts  6.19 us
  transfers between devices with their start and end apart: 7, of which 6 were waited for; matrix products, arithmetic and copies ran while one was open for 3% of the time, Pallas kernels for 0%

profile of v1, /device:TPU:101, one launch (start us, length us, event | category | flops | bytes accessed | tf_op | source)
XLA Modules:
  0.0 273.4 jit_solution(4701235985924256565)
XLA Ops:
  7.2 0.0 all-gather.7.cloned.1.call-start
  7.9 1.0 bitcast_select_fusion.2
  8.9 1.9 collective-permute-start
  10.8 20.4 %collective-permute-done = bf16[64,2048]{1,0:T(8,128)(2,1)S(1)} collective-permute-done((bf16[64,2048]{1,0:T(8,128)(2,1)S(1)}, bf16[64,2048]{1,0:T(8,128)(2,1)S(1)}, u32[]{:S(2)}, u32[]{:S(2)}) %collective-permute-start) | collective-permute-done | bytes 262176 | tf_op jit(solution)/shard_map/ppermute | solution.py:255
  31.3 0.0 copy-start.5
  31.3 0.7 copy-done.5
  32.0 0.0 all-gather.7.cloned.1.call-update
  32.0 0.0 all-gather.9.cloned.1.call-start
  32.0 0.7 all-gather.9.cloned.1.call-update
  32.7 0.0 all-gather.11.cloned.1.call-start
  32.8 0.7 all-gather.11.cloned.1.call-update
  33.5 0.7 iota_compare_fusion
  34.2 0.0 copy-start.2
  34.2 0.0 copy-start.3
  34.2 0.0 copy-start.4
  34.2 2.1 reduce-precision_convert_fusion
  36.4 71.6 %all-gather.7.cloned.1.call-done = bf16[1024,2048]{1,0:T(8,128)(2,1)} async-done(((bf16[64,2048]{1,0:T(8,128)(2,1)}), bf16[1024,2048]{1,0:T(8,128)(2,1)}) %all-gather.7.cloned.1.call-update) | async-done | bytes 4194320 | tf_op jit(solution)/shard_map/all_gather | solution.py:256
  108.0 3.7 %convolution_convert_fusion = bf16[2,512,64]{1,2,0:T(8,128)(2,1)S(1)} fusion(bf16[2,512,2048]{2,1,0:T(8,128)(2,1)} %bitcast.29, bf16[1,2,1,64,2048]{4,3,2,1,0:T(8,128)(2,1)} %param.12, pred[2,64]{1,0:T(4,128)(4,1)S(1)} %iota_compare_fusion), kind=kOutput, calls=%fused_computation | convolution fusion | flops 268763136 | bytes 4849792 | tf_op jit(solution)/shard_map/dot_general | solution.py:257
  111.7 0.2 reshape.57
  111.9 0.2 copy.14
  112.1 0.9 reshape.65
  113.0 6.7 %all-to-all-start = ((bf16[8,2,4096]{2,1,0:T(2,128)(2,1)}), bf16[8,2,4096]{2,1,0:T(2,128)(2,1)S(1)}, u32[]{:S(2)}, u32[]{:S(2)}) async-start(bf16[8,2,4096]{2,1,0:T(2,128)(2,1)} %reshape.65), calls=%async_computation | async-start | bytes 262144 | tf_op jit(solution)/shard_map/all_to_all | solution.py:261
  119.8 5.5 %all-to-all-done = bf16[8,2,4096]{2,1,0:T(2,128)(2,1)S(1)} async-done(((bf16[8,2,4096]{2,1,0:T(2,128)(2,1)}), bf16[8,2,4096]{2,1,0:T(2,128)(2,1)S(1)}, u32[]{:S(2)}, u32[]{:S(2)}) %all-to-all-start) | async-done | bytes 131104 | tf_op jit(solution)/shard_map/all_to_all | solution.py:261
  125.3 0.2 reshape.66
  125.5 40.6 %all-gather.9.cloned.1.call-done = bf16[1,16,1,64,2048]{4,3,2,0,1:T(8,128)(2,1)} async-done(((bf16[1,2,1,64,2048]{4,3,2,0,1:T(8,128)(2,1)}), bf16[1,16,1,64,2048]{4,3,2,0,1:T(8,128)(2,1)}) %all-gather.9.cloned.1.call-update) | async-done | bytes 4194320 | tf_op jit(solution)/shard_map/all_gather | solution.py:242
  166.2 56.3 %all-gather.11.cloned.1.call-done = bf16[16,1,1,64,2048]{4,3,2,1,0:T(8,128)(2,1)} async-done(((bf16[1,1,1,64,2048]{4,3,2,1,0:T(8,128)(2,1)}), bf16[16,1,1,64,2048]{4,3,2,1,0:T(8,128)(2,1)}) %all-gather.11.cloned.1.call-update) | async-done | bytes 4194320 | tf_op jit(solution)/shard_map/all_gather | solution.py:243
  222.5 0.0 copy-done.2
  222.5 0.0 copy-done.3
  222.5 0.0 copy-done.4
  222.5 0.0 copy-start
  222.5 2.2 copy-done
  224.7 0.0 copy-start.1
  224.7 2.2 copy-done.1
  226.9 20.7 %layer_update.1 = (f32[64,2048]{1,0:T(8,128)S(1)}, f32[64,2048]{1,0:T(8,128)S(1)}) custom-call(s32[6]{0:T(128)S(1)} %bitcast.28, f32[64,2048]{1,0:T(8,128)S(1)} %bitcast.26, f32[64,2048]{1,0:T(8,128)S(1)} %bitcast.27, bf16[16,64,64]{2,1,0:T(8,128)(2,1)S(1)} %bitcast.25, bf16[128,2048]{1,0:T(8,128)(2,1)S(1)} %pad_maximum_fusion.start, ...), custom_call_target="tpu_custom_call" | custom-call | tf_op jit(solution)/shard_map/layer_update/pallas_call | solution.py:184
  247.6 1.1 collective-permute-start.2
  248.7 0.1 collective-permute-start.1
  248.8 1.6 collective-permute-done.2
  250.4 1.1 broadcast_select_fusion
  251.6 0.0 collective-permute-done.1
  251.6 0.1 broadcast_select_fusion.2
  251.7 15.2 %join.1 = (f32[64,1024]{1,0:T(8,128)}, f32[64,1024]{1,0:T(8,128)}) custom-call(s32[1]{0:T(128)} %bitcast.offset, f32[64,2048]{1,0:T(8,128)S(1)} %get-tuple-element.13.probes_a, f32[64,2048]{1,0:T(8,128)S(1)} %get-tuple-element.12.probes_b, f32[64,2048]{1,0:T(8,128)S(1)} %get-tuple-element.11.images_a, f32[64,2048]{1,0:T(8,128)S(1)} %get-tuple-element.10.images_b, ...), custom_call_target="tpu_custom_call" | custom-call | tf_op jit(solution)/shard_map/join/pallas_call | solution.py:229
  (4 shorter events, 0.1 us)
Async XLA Ops:
  7.2 100.8 %all-gather.7.cloned.1.call-start = ((), (), s32[]{:S(2)}) async-start(), calls=%async_computation.1 | async-start | bytes 4456448 | tf_op jit(solution)/shard_map/all_gather | solution.py:256
  8.9 22.4 %collective-permute-start = (bf16[64,2048]{1,0:T(8,128)(2,1)S(1)}, bf16[64,2048]{1,0:T(8,128)(2,1)S(1)}, u32[]{:S(2)}, u32[]{:S(2)}) collective-permute-start(bf16[64,2048]{1,0:T(8,128)(2,1)S(1)} %bitcast_select_fusion.2), channel_id=1, source_target_pairs={{0,0},{2,16},{4,32},{6,48},{8,64},{10,80},{12,96},{14,112},{16,128... | collective-permute-start | bytes 786440 | tf_op jit(solution)/shard_map/ppermute | solution.py:255
  31.3 0.7 copy-start.5
  32.0 134.2 %all-gather.9.cloned.1.call-start = ((), (), s32[]{:S(2)}) async-start(), calls=%async_computation.2 | async-start | bytes 4718592 | tf_op jit(solution)/shard_map/all_gather | solution.py:242
  32.7 189.8 %all-gather.11.cloned.1.call-start = ((), (), s32[]{:S(2)}) async-start(), calls=%async_computation.3 | async-start | bytes 4456448 | tf_op jit(solution)/shard_map/all_gather | solution.py:243
  34.2 188.3 %copy-start.2 = (f32[1,1,64,2048]{3,2,1,0:T(8,128)S(1)}, f32[1,1,64,2048]{3,2,1,0:T(8,128)}, u32[]{:S(2)}) copy-start(f32[1,1,64,2048]{3,2,1,0:T(8,128)} %param.9) | copy-start | bytes 1572868
  34.2 188.3 %copy-start.3 = (f32[1,1,64,2048]{3,2,1,0:T(8,128)S(1)}, f32[1,1,64,2048]{3,2,1,0:T(8,128)}, u32[]{:S(2)}) copy-start(f32[1,1,64,2048]{3,2,1,0:T(8,128)} %param.10) | copy-start | bytes 1572868
  34.2 188.3 %copy-start.4 = (s32[1,1,1,6]{3,2,1,0:T(1,128)S(1)}, s32[1,1,1,6]{3,2,1,0:T(1,128)}, u32[]{:S(2)}) copy-start(s32[1,1,1,6]{3,2,1,0:T(1,128)} %param.17) | copy-start | bytes 76
  113.0 12.3 %all-to-all-start = ((bf16[8,2,4096]{2,1,0:T(2,128)(2,1)}), bf16[8,2,4096]{2,1,0:T(2,128)(2,1)S(1)}, u32[]{:S(2)}, u32[]{:S(2)}) async-start(bf16[8,2,4096]{2,1,0:T(2,128)(2,1)} %reshape.65), calls=%async_computation | async-start | bytes 262144 | tf_op jit(solution)/shard_map/all_to_all | solution.py:261
  222.5 2.2 copy-start
  224.7 2.2 copy-start.1
  247.6 2.8 %collective-permute-start.2 = (f32[64,2048]{1,0:T(8,128)S(1)}, f32[64,2048]{1,0:T(8,128)}, u32[]{:S(2)}, u32[]{:S(2)}) collective-permute-start(f32[64,2048]{1,0:T(8,128)S(1)} %get-tuple-element.7), channel_id=1, source_target_pairs={{0,1},{1,0},{2,3},{3,2},{4,5},{5,4},{6,7},{7,6},{8,9},{9,8},{10,11... | collective-permute-start | bytes 1572872 | tf_op jit(solution)/shard_map/ppermute | solution.py:272
  248.7 2.8 %collective-permute-start.1 = (f32[64,2048]{1,0:T(8,128)S(1)}, f32[64,2048]{1,0:T(8,128)S(1)}, u32[]{:S(2)}, u32[]{:S(2)}) collective-permute-start(f32[64,2048]{1,0:T(8,128)S(1)} %get-tuple-element.6), channel_id=1, source_target_pairs={{0,1},{1,0},{2,3},{3,2},{4,5},{5,4},{6,7},{7,6},{8,9},{9,8},{10,11... | collective-permute-start | bytes 1572872 | tf_op jit(solution)/shard_map/ppermute | solution.py:272
Sparse Core Ops, SparseCore 0:
  32.1 75.8 all-gather.6
  109.8 56.3 all-gather.8
  168.6 53.8 all-gather.10
